TPU v7x, 128 devices: a whole 4x4x4 slice. The times are simulated.
128 devices in a mesh: dp: 32 (over x, z, core), rep: 4 (over y).
Axes of the slice: x: 4, y: 4, z: 4, core: 2. Of those that a mesh axis runs over, the one named last changes fastest.
Arguments:
- cross_in: bfloat16 [65536, 3456], P(('dp', 'rep')), may hold values from -24 to 24
- cotangent: bfloat16 [65536, 3456], P(('dp', 'rep')), may hold values from -24 to 24
- weight_down: bfloat16 [3456, 512], replicated, may hold values from -0.109375 to 0.109375
- weight_up: bfloat16 [512, 3456], replicated, may hold values from -0.25 to 0.25
- cross_bias: float32 [3456], replicated, may hold values from -3 to 3
- row_place: int32 [65536, 26], P(('dp', 'rep')), may hold values from 0 to 66559, as said below
- frequent_table: float32 [1024, 128], replicated, may hold values from -0.6 to 0.6
- frequent_accum: float32 [1024], replicated, may hold values from 416 to 106496
- shard_table: float32 [65536, 128], P('dp'), may hold values from -0.6 to 0.6
- shard_accum: float32 [65536], P('dp'), may hold values from 0.01 to 1
Outputs:
- new_frequent: float32 [1024, 128], replicated
- new_frequent_accum: float32 [1024], replicated
- new_shard: float32 [65536, 128], P('dp')
- new_shard_accum: float32 [65536], P('dp')
- grad_up: float32 [512, 3456], P(('dp', 'rep'))
- grad_down: float32 [3456, 512], P(('dp', 'rep'))
- grad_bias: float32 [3456], P(('dp', 'rep'))
Inputs may be any that keep to these rules, and one draw needn't show every extreme that they name: `row_place`: within the rows of one device (aligned blocks of 512 samples), at most 208 entries name rows of any one owner, and in every block some owner is named by exactly 208 entries; every owner is named at least once in every block.
All inputs are finite; a program needn't handle non-finite values.
Results may differ from a plain program's by a relative error of at most 0.0013.
The roundings to bfloat16 on the way count: a program that leaves them out, or rounds other values in their place, can miss the bound.
Values sent between devices are 32-bit elements; how exact they have to be, the bound alone decides.
A program may use at most 192 MiB of HBM per device.

v0:
```python
import jax
import jax.numpy as jnp
from jax import lax
from jax.sharding import PartitionSpec as P

learn_rate = 0.05
eps_ada = 1e-08


def row_adagrad(table, accum, grad):
    accum_new = accum + jnp.mean(grad * grad, axis=1)
    return (table - learn_rate * grad / (jnp.sqrt(accum_new)[:, None] + eps_ada), accum_new)


def body(
    cross_in,
    cotangent,
    weight_down,
    weight_up,
    cross_bias,
    row_place,
    frequent_table,
    frequent_accum,
    shard_table,
    shard_accum,
):
    emb_width = frequent_table.shape[1]
    num_tables = row_place.shape[1]
    local_rows = cross_in.shape[0]
    f_count = frequent_table.shape[0]
    owned_rows = shard_table.shape[0]
    hidden = jnp.dot(cross_in, weight_down, preferred_element_type=jnp.float32).astype(jnp.bfloat16)
    scaled = jnp.dot(hidden, weight_up, preferred_element_type=jnp.float32) + cross_bias
    cot_wide = cotangent.astype(jnp.float32)
    inner = cot_wide * cross_in.astype(jnp.float32)
    inner_half = inner.astype(jnp.bfloat16)
    back_low = lax.dot_general(
        inner_half, weight_up, (((1,), (1,)), ((), ())), preferred_element_type=jnp.float32
    ).astype(jnp.bfloat16)
    back_in = cot_wide * (scaled + 1.0) + lax.dot_general(
        back_low, weight_down, (((1,), (1,)), ((), ())), preferred_element_type=jnp.float32
    )
    local_up = lax.dot_general(
        hidden, inner_half, (((0,), (0,)), ((), ())), preferred_element_type=jnp.float32
    )
    local_down = lax.dot_general(
        cross_in, back_low, (((0,), (0,)), ((), ())), preferred_element_type=jnp.float32
    )
    local_bias = jnp.sum(inner, axis=0)
    grad_up, grad_down, grad_bias = (
        lax.psum_scatter(local_up, ("dp", "rep"), scatter_dimension=0, tiled=True),
        lax.psum_scatter(local_down, ("dp", "rep"), scatter_dimension=0, tiled=True),
        lax.psum_scatter(local_bias, ("dp", "rep"), scatter_dimension=0, tiled=True),
    )
    values = back_in[:, emb_width:].reshape(local_rows * num_tables, emb_width)
    places = row_place.reshape(-1)
    is_frequent = places < f_count
    freq_grad = jax.ops.segment_sum(values, jnp.where(is_frequent, places, f_count), f_count + 1)[
        :f_count
    ]
    shards = lax.axis_size("dp")
    capacity = local_rows * num_tables // (2 * shards)
    owners = jnp.where(is_frequent, shards, (places - f_count) // owned_rows)
    owner_row = jnp.where(is_frequent, 0, (places - f_count) % owned_rows)
    sorted_order = jnp.argsort(owners, stable=True)
    sorted_owner = owners[sorted_order]
    counts = jnp.sum((owners[:, None] == jnp.arange(shards + 1)[None, :]).astype(jnp.int32), axis=0)
    starts = jnp.cumsum(counts) - counts
    slot_pos = jnp.arange(owners.shape[0]) - starts[sorted_owner]
    target = jnp.where(sorted_owner < shards, sorted_owner * capacity + slot_pos, shards * capacity)
    bucket = (
        jnp.zeros((shards * capacity + 1, emb_width), jnp.float32)
        .at[target]
        .set(values[sorted_order])
    )
    bucket = bucket[: shards * capacity].reshape(shards, capacity, emb_width)
    bucket_rows = (
        jnp.zeros((shards * capacity + 1,), jnp.int32).at[target].set(owner_row[sorted_order])
    )
    bucket_rows = bucket_rows[: shards * capacity].reshape(shards, capacity)
    arrived, arrived_rows = (
        lax.all_to_all(bucket, "dp", split_axis=0, concat_axis=0, tiled=True),
        lax.all_to_all(bucket_rows, "dp", split_axis=0, concat_axis=0, tiled=True),
    )
    shard_grad = jax.ops.segment_sum(
        arrived.reshape(-1, emb_width), arrived_rows.reshape(-1), owned_rows
    )
    shard_grad = lax.psum(shard_grad, "rep")
    new_shard, new_shard_accum = row_adagrad(shard_table, shard_accum, shard_grad)
    freq_total = lax.psum(freq_grad, ("dp", "rep"))
    new_frequent, new_frequent_accum = row_adagrad(frequent_table, frequent_accum, freq_total)
    return (
        new_frequent,
        new_frequent_accum,
        new_shard,
        new_shard_accum,
        grad_up,
        grad_down,
        grad_bias,
    )


def solution(mesh):
    in_specs = (
        P(("dp", "rep"), None),
        P(("dp", "rep"), None),
        P(),
        P(),
        P(),
        P(("dp", "rep"), None),
        P(),
        P(),
        P("dp", None),
        P("dp"),
    )
    out_specs = (
        P(),
        P(),
        P("dp", None),
        P("dp"),
        P(("dp", "rep"), None),
        P(("dp", "rep"), None),
        P(("dp", "rep")),
    )
    return jax.shard_map(body, mesh=mesh, in_specs=in_specs, out_specs=out_specs, check_vma=False)
```

profile of v0, /device:TPU:1, one launch (start us, length us, event | category | flops | bytes accessed | tf_op | source)
XLA Modules:
  0.0 876.3 jit_solution(13880018079292635862)
XLA Ops:
  11.3 1.8 sub.33
  22.4 9.1 %sort.17 = (s32[13312]{0:T(1024)}, s32[13312]{0:T(1024)}) sort(s32[13312]{0:T(1024)} %copy-done.2, s32[13312]{0:T(1024)} %iota.12), dimensions={0}, to_apply=%region_3.0 | sort | flops 186368 | bytes 212992 | tf_op jit(solution)/shard_map/jit(argsort)/sort | solution.py:65
  32.9 121.2 %gather_fusion = s32[13312]{0:T(1024)} fusion(s32[13312]{0:T(1024)} %copy-done.2, s32[13312]{0:T(1024)} %fusion.19), kind=kCustom, calls=%fused_computation | custom fusion | bytes 159744 | tf_op jit(solution)/shard_map/gather | solution.py:66
  154.1 5.3 compare_select_fusion.3
  159.4 4.2 compare_reduce_fusion.25
  163.7 16.6 %select_select_fusion = s32[13312]{0:T(1024)S(1)} fusion(pred[13312]{0:T(1024)(128)(4,1)S(1)} %get-tuple-element.62, pred[13312]{0:T(1024)(128)(4,1)S(1)} %get-tuple-element.61, pred[13312]{0:T(1024)(128)(4,1)S(1)} %get-tuple-element.60, pred[13312]{0:T(1024)(128)(4,1)S(1)} %get-tuple-element.59, pred[13312]{0:T(1024)(128)(4,1)S(1)} %get-tuple-element.58, ...), kind=kLoop, calls=%fused_computation.77 | loop fusion | flops 346112 | bytes 452712 | tf_op jit(solution)/shard_map/gather | solution.py:69
  181.8 120.7 %gather_fusion.1 = s32[13312]{0:T(1024)} fusion(s32[13312]{0:T(1024)} %get-tuple-element.72, s32[13312]{0:T(1024)} %fusion.19), kind=kCustom, calls=%fused_computation.1 | custom fusion | bytes 159744 | tf_op jit(solution)/shard_map/gather | solution.py:78
  302.6 49.8 %scatter_custom_fusion.1 = s32[6657]{0:T(1024)} fusion(s32[13312]{0:T(1024)} %bitcast.62, s32[13312]{0:T(1024)} %gather_fusion.1, s32[]{:T(128)} %constant.29.clone.1), kind=kCustom, calls=%fused_computation.83 | custom fusion | bytes 27140 | tf_op jit(solution)/shard_map/scatter | solution.py:78
  353.9 9.8 %all-to-all-start = ((s32[32,1,208]{2,1,0:T(1,128)}), s32[32,1,208]{2,1,0:T(1,128)}, u32[]{:S(2)}, u32[]{:S(2)}) async-start(s32[32,1,208]{2,1,0:T(1,128)} %all_to_all.9), calls=%async_computation | async-start | bytes 65536 | tf_op jit(solution)/shard_map/all_to_all | solution.py:83
  363.7 2.6 convert_element_type.18
  367.9 2.0 convolution_convert_fusion
  369.9 2.1 fusion.10
  372.1 2.1 fusion.26
  374.3 2.1 fusion.27
  376.4 3.3 slice_add_fusion
  379.7 7.8 reshape.231
  387.5 108.6 %scatter_custom_fusion.2 = f32[6657,128]{1,0:T(8,128)S(1)} fusion(s32[13312]{0:T(1024)} %bitcast.63, f32[13312,128]{1,0:T(8,128)} %reshape.231, s32[13312]{0:T(1024)} %fusion.19, f32[]{:T(128)} %constant.21.clone.1), kind=kCustom, calls=%fused_computation.12 | custom fusion | bytes 3408896 | tf_op jit(solution)/shard_map/scatter | solution.py:74
  496.1 2.1 slice.62
  498.2 7.8 all-to-all-start.1
  507.8 1.8 reshape.157
  511.1 72.4 %scatter_custom_fusion = f32[1025,128]{1,0:T(8,128)} fusion(s32[13312]{0:T(1024)} %bitcast.64, f32[13312,128]{1,0:T(8,128)} %reshape.231, f32[]{:T(128)} %constant.21.clone.1), kind=kCustom, calls=%fused_computation.33 | custom fusion | flops 1703936 | bytes 525312 | tf_op jit(solution)/shard_map/scatter-add | solution.py:58
  583.4 1.9 slice.60
  588.2 41.0 %scatter_custom_fusion.3 = f32[2048,128]{1,0:T(8,128)} fusion(s32[6656]{0:T(1024)} %reshape.253, f32[6656,128]{1,0:T(8,128)} %bitcast.40, f32[]{:T(128)} %constant.21.clone.1), kind=kCustom, calls=%fused_computation.26 | custom fusion | flops 851968 | bytes 1049088 | tf_op jit(solution)/shard_map/scatter-add | solution.py:85
  629.4 6.2 convolution_bitcast_fusion
  635.6 5.1 fusion.6
  640.7 4.2 fusion.3
  644.8 67.5 %all-reduce.2 = f32[3456]{0:T(1024)} all-reduce(f32[3456]{0:T(1024)S(1)} %fusion.3), channel_id=4, replica_groups=mesh['dp'=32,'rep'=4] {'dp','rep'}, use_global_device_ids=true, to_apply=%region_14.15.clone | all-reduce | flops 3456 | bytes 27648
  716.5 3.0 divide_subtract_fusion
  719.4 140.0 %all-reduce.9.cloned.1.call-done = (f32[1024,128]{1,0:T(8,128)}, f32[512,3456]{1,0:T(8,128)}, f32[3456,512]{0,1:T(8,128)}) async-done(((f32[1024,128]{1,0:T(8,128)}, f32[512,3456]{1,0:T(8,128)}, f32[3456,512]{0,1:T(8,128)}), (f32[1024,128]{1,0:T(8,128)}, f32[512,3456]{1,0:T(8,128)}, f32[3456,512]{0,1:T(8,128)})) %all-reduce.9.cloned.1.call-update) | async-done | bytes 14680080 | tf_op jit(solution)/shard_map/psum | solution.py:90
  860.7 1.9 constant_dynamic-slice_fusion
  862.6 1.7 copy.33
  865.5 2.2 divide_subtract_fusion.1
  (61 shorter events, 34.0 us)
Async XLA Ops:
  7.2 362.8 %copy-start = (bf16[512,3456]{1,0:T(8,128)(2,1)S(1)}, bf16[512,3456]{1,0:T(8,128)(2,1)}, u32[]{:S(2)}) copy-start(bf16[512,3456]{1,0:T(8,128)(2,1)} %param.13) | copy-start | bytes 10616836
  16.4 0.6 copy-start.2
  353.9 144.3 %all-to-all-start = ((s32[32,1,208]{2,1,0:T(1,128)}), s32[32,1,208]{2,1,0:T(1,128)}, u32[]{:S(2)}, u32[]{:S(2)}) async-start(s32[32,1,208]{2,1,0:T(1,128)} %all_to_all.9), calls=%async_computation | async-start | bytes 65536 | tf_op jit(solution)/shard_map/all_to_all | solution.py:83
  363.7 3.1 copy-start.3
  363.7 4.1 copy-start.7
  367.9 2.1 copy-start.5
  369.9 2.1 copy-start.9
  372.1 4.3 copy-start.11
  372.1 2.2 copy-start.8
  374.3 2.1 copy-start.12
  498.2 131.1 %copy-start.4 = (bf16[512,3456]{1,0:T(8,128)(2,1)S(1)}, bf16[512,3456]{1,0:T(8,128)(2,1)}, u32[]{:S(2)}) copy-start(bf16[512,3456]{1,0:T(8,128)(2,1)} %param.10) | copy-start | bytes 10616836
  498.2 90.0 %all-to-all-start.1 = ((f32[32,208,128]{2,1,0:T(8,128)}), f32[32,208,128]{2,1,0:T(8,128)}, u32[]{:S(2)}, u32[]{:S(2)}) async-start(f32[32,208,128]{2,1,0:T(8,128)} %bitcast.56), calls=%async_computation.1 | async-start | bytes 6815744 | tf_op jit(solution)/shard_map/all_to_all | solution.py:82
  506.1 207.5 %all-reduce.7.cloned.1.call-start = ((), (), s32[]{:S(2)}) async-start(), calls=%async_computation.2 | async-start | bytes 2097152 | tf_op jit(solution)/shard_map/psum | solution.py:88
  629.3 230.1 %all-reduce.9.cloned.1.call-start = ((), (), s32[]{:S(2)}) async-start(), calls=%async_computation.3 | async-start | bytes 29360128 | tf_op jit(solution)/shard_map/psum | solution.py:90
  629.3 6.2 copy-start.6
  629.4 6.2 copy-start.10
  640.7 228.6 %copy-start.1 = (bf16[512,3456]{1,0:T(8,128)(2,1)S(1)}, bf16[512,3456]{1,0:T(8,128)(2,1)}, u32[]{:S(2)}) copy-start(bf16[512,3456]{1,0:T(8,128)(2,1)} %param.13) | copy-start | bytes 10616836
Sparse Core Ops, SparseCore 0:
  629.4 46.4 all-reduce.6
  683.0 176.4 all-reduce.8
where the time goes:
time: 884 us; the launch traced here: 876 us
  local copies, waits for them, and re-layouts  435 us (49%)
  other arithmetic  182 us (21%)
  waiting for transfers between devices  140 us (16%)
  blocking collectives  67.5 us (8%)
  matrix products  19.6 us (2%)
  starting transfers between devices  17.8 us (2%)
  between operations  14.5 us (2%)
    psum x1, waiting for transfers between devices, body(): freq_total = lax.psum(freq_grad, ('dp', 'rep'))  140 us
    gather x1, local copies, waits for them, and re-layouts, body(): sorted_owner = owners[sorted_order]  121 us
    gather x1, local copies, waits for them, and re-layouts, body(): owner_row[sorted_order]  121 us
    scatter x1, local copies, waits for them, and re-layouts, body(): bucket = jnp.zeros((shards * capacity + 1, emb_width), jnp.float32).at[ta...  109 us
    scatter-add x1, other arithmetic, body(): jax.ops.segment_sum(values, jnp.where(is_frequent, places, f_count), f_co...  72.4 us
    unnamed x1, blocking collectives  67.5 us
    scatter x1, local copies, waits for them, and re-layouts, body(): jnp.zeros((shards * capacity + 1,), jnp.int32).at[target]  49.8 us
    scatter-add x1, other arithmetic, body(): jax.ops.segment_sum(arrived.reshape(-1, emb_width), arrived_rows.reshape(...  41 us
  transfers between devices with their start and end apart: 4, of which 1 were waited for; matrix products, arithmetic and copies ran while one was open for 27% of the time, Pallas kernels for 0%

commit v1 on v0

--- a/solution.py
+++ b/solution.py
@@ -87,7 +87,8 @@
     )
     shard_grad = lax.psum(shard_grad, "rep")
     new_shard, new_shard_accum = row_adagrad(shard_table, shard_accum, shard_grad)
-    freq_total = lax.psum(freq_grad, ("dp", "rep"))
+    one_axis = lax.psum(freq_grad, "rep")
+    freq_total = lax.psum(one_axis, "dp")
     new_frequent, new_frequent_accum = row_adagrad(frequent_table, frequent_accum, freq_total)
     return (
         new_frequent,

time: 884 us -> 987 us (1.12)
  waiting for transfers between devices: 140 us -> 243 us
    unnamed x2 -> x4, waiting for transfers between devices: 0.03 us -> 173 us
    psum x2, waiting for transfers between devices: 140 us -> 69.7 us  [the longest x1 45.3 us: body(): one_axis = lax.psum(freq_grad, 'rep')]
  transfers between devices with their start and end apart: 4 -> 5, of which waited for: 1 -> 3; matrix products, arithmetic and copies ran while one was open for 27% -> 25% of each run, Pallas kernels for 0% -> 0%
where the time goes in v1:
time: 987 us; the launch traced here: 979 us
  local copies, waits for them, and re-layouts  435 us (44%)
  waiting for transfers between devices  243 us (25%)
  other arithmetic  182 us (18%)
  blocking collectives  65.6 us (7%)
  matrix products  21.6 us (2%)
  starting transfers between devices  17.8 us (2%)
  between operations  14.2 us (1%)
    unnamed x4, waiting for transfers between devices  173 us
    gather x1, local copies, waits for them, and re-layouts, body(): sorted_owner = owners[sorted_order]  121 us
    gather x1, local copies, waits for them, and re-layouts, body(): owner_row[sorted_order]  121 us
    scatter x1, local copies, waits for them, and re-layouts, body(): bucket = jnp.zeros((shards * capacity + 1, emb_width), jnp.float32).at[ta...  109 us
    scatter-add x1, other arithmetic, body(): jax.ops.segment_sum(values, jnp.where(is_frequent, places, f_count), f_co...  72.4 us
    unnamed x1, blocking collectives  65.6 us
    scatter x1, local copies, waits for them, and re-layouts, body(): jnp.zeros((shards * capacity + 1,), jnp.int32).at[target]  49.8 us
    psum x1, waiting for transfers between devices, body(): one_axis = lax.psum(freq_grad, 'rep')  45.3 us
  transfers between devices with their start and end apart: 5, of which 3 were waited for; matrix products, arithmetic and copies ran while one was open for 25% of the time, Pallas kernels for 0%

profile of v1, /device:TPU:1, one launch (start us, length us, event | category | flops | bytes accessed | tf_op | source)
XLA Modules:
  0.0 979.0 jit_solution(15853619704225845333)
XLA Ops:
  22.4 9.1 sort.17
  32.9 121.2 %gather_fusion = s32[13312]{0:T(1024)} fusion(s32[13312]{0:T(1024)} %copy-done.2, s32[13312]{0:T(1024)} %fusion.19), kind=kCustom, calls=%fused_computation | custom fusion | bytes 159744 | tf_op jit(solution)/shard_map/gather | solution.py:66
  154.1 5.3 compare_select_fusion.3
  159.4 4.2 compare_reduce_fusion.25
  163.7 16.6 %select_select_fusion = s32[13312]{0:T(1024)S(1)} fusion(pred[13312]{0:T(1024)(128)(4,1)S(1)} %get-tuple-element.62, pred[13312]{0:T(1024)(128)(4,1)S(1)} %get-tuple-element.61, pred[13312]{0:T(1024)(128)(4,1)S(1)} %get-tuple-element.60, pred[13312]{0:T(1024)(128)(4,1)S(1)} %get-tuple-element.59, pred[13312]{0:T(1024)(128)(4,1)S(1)} %get-tuple-element.58, ...), kind=kLoop, calls=%fused_computation.77 | loop fusion | flops 346112 | bytes 452712 | tf_op jit(solution)/shard_map/gather | solution.py:69
  181.8 120.7 %gather_fusion.1 = s32[13312]{0:T(1024)} fusion(s32[13312]{0:T(1024)} %get-tuple-element.73, s32[13312]{0:T(1024)} %fusion.19), kind=kCustom, calls=%fused_computation.1 | custom fusion | bytes 159744 | tf_op jit(solution)/shard_map/gather | solution.py:78
  302.6 49.8 %scatter_custom_fusion.1 = s32[6657]{0:T(1024)} fusion(s32[13312]{0:T(1024)} %bitcast.62, s32[13312]{0:T(1024)} %gather_fusion.1, s32[]{:T(128)} %constant.29.clone.1), kind=kCustom, calls=%fused_computation.83 | custom fusion | bytes 27140 | tf_op jit(solution)/shard_map/scatter | solution.py:78
  353.9 9.8 %all-to-all-start = ((s32[32,1,208]{2,1,0:T(1,128)}), s32[32,1,208]{2,1,0:T(1,128)}, u32[]{:S(2)}, u32[]{:S(2)}) async-start(s32[32,1,208]{2,1,0:T(1,128)} %all_to_all.9), calls=%async_computation | async-start | bytes 65536 | tf_op jit(solution)/shard_map/all_to_all | solution.py:83
  363.7 2.6 convert_element_type.18
  367.9 2.0 convolution_convert_fusion
  369.9 2.1 fusion.10
  372.1 2.1 fusion.26
  374.3 2.1 fusion.27
  376.4 3.3 slice_add_fusion
  379.7 7.8 reshape.231
  387.5 108.6 %scatter_custom_fusion.2 = f32[6657,128]{1,0:T(8,128)S(1)} fusion(s32[13312]{0:T(1024)} %bitcast.63, f32[13312,128]{1,0:T(8,128)} %reshape.231, s32[13312]{0:T(1024)} %fusion.19, f32[]{:T(128)} %constant.21.clone.1), kind=kCustom, calls=%fused_computation.12 | custom fusion | bytes 3408896 | tf_op jit(solution)/shard_map/scatter | solution.py:74
  496.1 2.1 slice.62
  498.2 7.8 all-to-all-start.1
  507.8 1.8 reshape.157
  511.1 72.4 %scatter_custom_fusion = f32[1025,128]{1,0:T(8,128)} fusion(s32[13312]{0:T(1024)} %bitcast.64, f32[13312,128]{1,0:T(8,128)} %reshape.231, f32[]{:T(128)} %constant.21.clone.1), kind=kCustom, calls=%fused_computation.33 | custom fusion | flops 1703936 | bytes 525312 | tf_op jit(solution)/shard_map/scatter-add | solution.py:58
  583.4 1.9 slice.60
  588.2 41.0 %scatter_custom_fusion.3 = f32[2048,128]{1,0:T(8,128)} fusion(s32[6656]{0:T(1024)} %reshape.253, f32[6656,128]{1,0:T(8,128)} %bitcast.40, f32[]{:T(128)} %constant.21.clone.1), kind=kCustom, calls=%fused_computation.26 | custom fusion | flops 851968 | bytes 1049088 | tf_op jit(solution)/shard_map/scatter-add | solution.py:85
  629.3 7.2 fusion.6
  636.5 45.3 %all-reduce.13.cloned.1.call-done = (f32[1024,128]{1,0:T(8,128)}, f32[2048,128]{1,0:T(8,128)}) async-done(((f32[1024,128]{1,0:T(8,128)}, f32[2048,128]{1,0:T(8,128)}), (f32[1024,128]{1,0:T(8,128)}, f32[2048,128]{1,0:T(8,128)})) %all-reduce.13.cloned.1.call-update) | async-done | bytes 1572880 | tf_op jit(solution)/shard_map/psum | solution.py:90
  681.9 6.1 convolution_bitcast_fusion
  688.1 4.2 fusion.3
  692.2 65.6 %all-reduce.2 = f32[3456]{0:T(1024)} all-reduce(f32[3456]{0:T(1024)S(1)} %fusion.3), channel_id=4, replica_groups=mesh['dp'=32,'rep'=4] {'dp','rep'}, use_global_device_ids=true, to_apply=%region_15.16.clone | all-reduce | flops 3456 | bytes 27648
  762.0 2.9 divide_subtract_fusion
  764.8 24.4 %all-reduce.9.cloned.1.call-done = f32[1024,128]{1,0:T(8,128)} async-done(((f32[1024,128]{1,0:T(8,128)}), f32[1024,128]{1,0:T(8,128)}) %all-reduce.9.cloned.1.call-update) | async-done | bytes 524304 | tf_op jit(solution)/shard_map/psum | solution.py:91
  791.8 2.2 divide_subtract_fusion.1
  794.0 173.2 %all-reduce.11.cloned.1.call-done = (f32[512,3456]{1,0:T(8,128)}, f32[3456,512]{0,1:T(8,128)}) async-done(((f32[512,3456]{1,0:T(8,128)}, f32[3456,512]{0,1:T(8,128)}), (f32[512,3456]{1,0:T(8,128)}, f32[3456,512]{0,1:T(8,128)})) %all-reduce.11.cloned.1.call-update) | async-done | bytes 14155792
  967.2 1.9 constant_dynamic-slice_fusion
  (60 shorter events, 37.5 us)
Async XLA Ops:
  7.2 362.8 %copy-start = (bf16[512,3456]{1,0:T(8,128)(2,1)S(1)}, bf16[512,3456]{1,0:T(8,128)(2,1)}, u32[]{:S(2)}) copy-start(bf16[512,3456]{1,0:T(8,128)(2,1)} %param.13) | copy-start | bytes 10616836
  16.4 0.6 copy-start.2
  353.9 144.3 %all-to-all-start = ((s32[32,1,208]{2,1,0:T(1,128)}), s32[32,1,208]{2,1,0:T(1,128)}, u32[]{:S(2)}, u32[]{:S(2)}) async-start(s32[32,1,208]{2,1,0:T(1,128)} %all_to_all.9), calls=%async_computation | async-start | bytes 65536 | tf_op jit(solution)/shard_map/all_to_all | solution.py:83
  363.7 3.1 copy-start.3
  363.7 4.1 copy-start.6
  367.9 2.1 copy-start.5
  369.9 2.1 copy-start.8
  372.1 4.3 copy-start.9
  372.1 2.2 copy-start.7
  374.3 2.1 copy-start.10
  498.2 131.1 %copy-start.4 = (bf16[512,3456]{1,0:T(8,128)(2,1)S(1)}, bf16[512,3456]{1,0:T(8,128)(2,1)}, u32[]{:S(2)}) copy-start(bf16[512,3456]{1,0:T(8,128)(2,1)} %param.10) | copy-start | bytes 10616836
  498.2 90.0 %all-to-all-start.1 = ((f32[32,208,128]{2,1,0:T(8,128)}), f32[32,208,128]{2,1,0:T(8,128)}, u32[]{:S(2)}, u32[]{:S(2)}) async-start(f32[32,208,128]{2,1,0:T(8,128)} %bitcast.56), calls=%async_computation.1 | async-start | bytes 6815744 | tf_op jit(solution)/shard_map/all_to_all | solution.py:82
  506.1 175.8 %all-reduce.13.cloned.1.call-start = ((), (), s32[]{:S(2)}) async-start(), calls=%async_computation.4 | async-start | bytes 3145728 | tf_op jit(solution)/shard_map/psum | solution.py:90
  629.3 160.0 %all-reduce.9.cloned.1.call-start = ((), (), s32[]{:S(2)}) async-start(), calls=%async_computation.2 | async-start | bytes 1048576 | tf_op jit(solution)/shard_map/psum | solution.py:91
  681.9 285.3 %all-reduce.11.cloned.1.call-start = ((), (), s32[]{:S(2)}) async-start(), calls=%async_computation.3 | async-start | bytes 28311552
  688.0 284.2 %copy-start.1 = (bf16[512,3456]{1,0:T(8,128)(2,1)S(1)}, bf16[512,3456]{1,0:T(8,128)(2,1)}, u32[]{:S(2)}) copy-start(bf16[512,3456]{1,0:T(8,128)(2,1)} %param.13) | copy-start | bytes 10616836
Sparse Core Ops, SparseCore 0:
  629.4 52.4 all-reduce.12
  685.1 104.1 all-reduce.8
  795.2 171.9 all-reduce.10
